TPU v7x, 256 devices: a whole 4x4x8 slice. The times are simulated.
256 devices in a mesh: group: 8 (over x, core), expert: 32 (over y, z).
Axes of the slice: x: 4, y: 4, z: 8, core: 2. Of those that a mesh axis runs over, the one named last changes fastest.
Arguments:
- resid: bfloat16 [32768, 2048], P(('group', 'expert')), may hold values from -6 to 6
- queries: bfloat16 [32768, 2048], P(('group', 'expert')), may hold values from -48 to 48
- span_kv: bfloat16 [2, 32768, 2048], P(None, ('group', 'expert')), may hold values from -4 to 4
- cache_kv: bfloat16 [2, 256, 2, 128, 2048], P(None, ('group', 'expert')), may hold values from -6 to 6
- seg_len: int32 [256, 2], P(('group', 'expert')), may hold values from 0 to 128, as said below
- o_rows: bfloat16 [2048, 2048], P('expert'), may hold values from -0.125 to 0.125
- norm_gain: float32 [2048], replicated, may hold values from 0.25 to 1.75
- routes: int32 [32768, 8], P(('group', 'expert')), may hold values from 0 to 31, all different within a row; in each aligned block of 128 rows (0 to 127, 128 to 255, ...) at most 48 rows name the same one
- route_wts: float32 [32768, 8], P(('group', 'expert')), may hold values from 0.05 to 0.6
- w_in: bfloat16 [32, 2048, 1024], P('expert'), may hold values from -0.125 to 0.125
- w_out: bfloat16 [32, 512, 2048], P('expert'), may hold values from -0.25 to 0.25
Outputs:
- layer_out: bfloat16 [32768, 2048], P(('group', 'expert'))
Inputs may be any that keep to these rules, and one draw needn't show every extreme that they name: seg_len[d, 0] is 1 to 128; seg_len[d, 1] is 0 (the paired request is short) or 1 to 128; seg_len[0, 0] and seg_len[0, 1] are 128 and seg_len[1, 1] is 0. `routes`: each row names 8 different experts; among the 128 rows of one device no expert is named more than 48 times.
All inputs are finite; a program needn't handle non-finite values.
Results may differ from a plain program's by a relative error of at most 0.0053.
Values may be sent and summed in bfloat16 or wider, within the bound.
A program may use at most 128 MiB of HBM per device.

v0:
```python
import math
import jax
import jax.numpy as jnp
from jax import lax
from jax.sharding import PartitionSpec as P

HEADS = 16
HD = 128
FF = 512
TOPK = 8


def swapped(block, axis, distance):
    count = lax.axis_size(axis)
    route = []
    for low in range(count):
        high = low | 1 << distance
        if high != low and high < count:
            route += [(low, high), (high, low)]
    return lax.ppermute(block, axis, route)


def attend(query_rows, key_rows, value_rows, valid_keys):
    q_heads = query_rows.reshape(query_rows.shape[0], HEADS, HD)
    k_heads = key_rows.reshape(key_rows.shape[0], HEADS, HD)
    v_heads = value_rows.reshape(value_rows.shape[0], HEADS, HD)
    scores = jnp.einsum("chd,shd->hcs", q_heads, k_heads, preferred_element_type=jnp.float32) * (
        1.0 / math.sqrt(HD)
    )
    scores = jnp.where(valid_keys[None, None, :], scores, -1e30)
    peak_score = jnp.max(scores, axis=-1)
    expo = jnp.where(valid_keys[None, None, :], jnp.exp(scores - peak_score[..., None]), 0.0)
    totals = jnp.sum(expo, axis=-1)
    probs_low = expo.astype(jnp.bfloat16)
    accum_out = jnp.einsum("hcs,shd->chd", probs_low, v_heads, preferred_element_type=jnp.float32)
    return (peak_score, totals, accum_out)


def merge_parts(first, second):
    peak_a, total_a, accum_a = first
    peak_b, total_b, accum_b = second
    peak_both = jnp.maximum(peak_a, peak_b)
    scale_a = jnp.exp(peak_a - peak_both).T
    scale_b = jnp.exp(peak_b - peak_both).T
    numer = accum_a * scale_a[:, :, None] + accum_b * scale_b[:, :, None]
    denom = total_a.T * scale_a + total_b.T * scale_b
    merged = numer / denom[:, :, None]
    return merged.reshape(merged.shape[0], -1).astype(jnp.bfloat16)


def expert_mlp(token_rows, weight_in, weight_out):
    joined = jnp.dot(token_rows, weight_in, preferred_element_type=jnp.float32)
    hidden = (jax.nn.silu(joined[:, :FF]) * joined[:, FF:]).astype(jnp.bfloat16)
    return jnp.dot(hidden, weight_out, preferred_element_type=jnp.float32).astype(jnp.bfloat16)


def shards(
    resid, queries, span_kv, cache_kv, seg_len, o_rows, norm_gain, routes, route_wts, w_in, w_out
):
    span_rows = queries.shape[0]
    seg_rows = cache_kv.shape[3]
    width = queries.shape[1]
    experts_here = lax.axis_size("expert")
    positions = jnp.arange(seg_rows, dtype=jnp.int32)
    keys_a = jnp.concatenate([span_kv[0], cache_kv[0, 0, 0]], axis=0)
    vals_a = jnp.concatenate([span_kv[1], cache_kv[1, 0, 0]], axis=0)
    valid_a = jnp.concatenate([jnp.ones((span_rows,), bool), positions < seg_len[0, 0]])
    part_a = attend(queries, keys_a, vals_a, valid_a)
    length_low = seg_len[0, 1:2].astype(jnp.float32).astype(jnp.bfloat16)
    fetched, fetched_len = swapped((cache_kv[:, 0, 1], length_low), "group", 0)
    valid_b = positions.astype(jnp.float32) < fetched_len[0].astype(jnp.float32)
    part_b = attend(queries, fetched[0], fetched[1], valid_b)
    attended = merge_parts(part_a, part_b)
    projected = jnp.dot(
        attended,
        lax.all_gather(o_rows, "expert", axis=0, tiled=True),
        preferred_element_type=jnp.float32,
    )
    residual = resid.astype(jnp.float32) + projected
    normed = (
        residual
        * lax.rsqrt(jnp.mean(residual * residual, axis=-1, keepdims=True) + 1e-05)
        * norm_gain
    ).astype(jnp.bfloat16)
    capacity = min(span_rows, span_rows * TOPK * 3 // (2 * experts_here))
    onehot = (
        routes[:, :, None] == jnp.arange(experts_here, dtype=jnp.int32)[None, None, :]
    ).astype(jnp.int32)
    counts = jnp.sum(onehot, axis=1)
    before = jnp.cumsum(counts, axis=0) - counts
    slot_ids = jnp.sum(onehot * before[:, None, :], axis=-1)
    flat_slot = routes * capacity + slot_ids
    placing = jnp.any(
        flat_slot[None, :, :]
        == jnp.arange(experts_here * capacity, dtype=jnp.int32)[:, None, None],
        axis=-1,
    )
    outgoing = jnp.dot(
        placing.astype(jnp.bfloat16), normed, preferred_element_type=jnp.float32
    ).astype(jnp.bfloat16)
    outgoing = outgoing.reshape(experts_here, capacity, width)
    arrived = lax.all_to_all(outgoing, "expert", split_axis=0, concat_axis=0, tiled=True)
    flat_rows = arrived.reshape(-1, width)
    output_rows = expert_mlp(flat_rows, w_in[0], w_out[0]).reshape(arrived.shape)
    returned_rows = lax.all_to_all(output_rows, "expert", split_axis=0, concat_axis=0, tiled=True)
    returned_rows = returned_rows.reshape(experts_here * capacity, width)
    expert_sum = jnp.zeros((span_rows, width), jnp.float32)
    for route_k in range(TOPK):
        picked = returned_rows[flat_slot[:, route_k]].astype(jnp.float32)
        expert_sum = expert_sum + route_wts[:, route_k, None] * picked
    return (residual + expert_sum).astype(jnp.bfloat16)


def solution(mesh):
    placed = (
        P(("group", "expert"), None),
        P(("group", "expert"), None),
        P(None, ("group", "expert"), None),
        P(None, ("group", "expert"), None, None, None),
        P(("group", "expert"), None),
        P("expert", None),
        P(),
        P(("group", "expert"), None),
        P(("group", "expert"), None),
        P("expert", None, None),
        P("expert", None, None),
    )
    return jax.shard_map(
        shards, mesh=mesh, in_specs=placed, out_specs=P(("group", "expert"), None), check_vma=False
    )
```

profile of v0, /device:TPU:33, one launch (start us, length us, event | category | flops | bytes accessed | tf_op | source)
XLA Modules:
  0.0 479.4 jit_solution(5816244615594503621)
XLA Ops:
  6.5 0.0 copy-start
  6.5 0.0 all-gather.2.cloned.1.call-start
  6.5 0.7 all-gather.2.cloned.1.call-update
  7.3 1.3 fusion.66
  9.2 1.6 collective-permute-start
  10.8 1.3 slice.87
  12.1 1.3 copy.55
  13.4 0.0 collective-permute-start.1
  13.4 2.1 fusion.65
  15.5 1.3 copy.53
  16.8 1.1 copy.39
  17.9 0.0 copy-start.6
  17.9 2.3 fusion.63
  20.2 1.3 copy.54
  21.5 1.1 copy.40
  22.6 1.0 copy.35
  23.6 2.1 copy.36
  25.7 0.0 copy-done.6
  25.7 0.1 copy.47
  25.8 0.2 reduce_window_sum.11
  26.0 0.1 copy.49
  26.1 0.6 iota_compare_fusion.2
  26.8 5.6 %fusion = pred[1536,128]{1,0:T(8,128)(4,1)S(1)} fusion(s32[128,8]{0,1:T(8,128)S(1)} %multiply_add_fusion), kind=kLoop, calls=%fused_computation.11 | loop fusion | flops 2949120 | bytes 200704 | tf_op jit(solution)/shard_map/reduce_or | solution.py:93
  32.4 1.9 bitcast_reduce_fusion
  34.2 0.0 copy-start.1
  34.2 0.0 copy-start.3
  34.2 1.3 copy-done.1
  35.6 0.6 fusion.9
  36.2 0.0 copy-start.4
  36.2 0.0 collective-permute-done
  36.9 0.0 copy-start.2
  36.9 0.0 copy-start.5
  37.0 0.0 collective-permute-done.1
  37.0 1.4 fusion.64
  38.4 0.0 copy-done.3
  38.4 0.5 fusion.67
  39.0 0.2 fusion.31
  39.2 0.0 copy-done.4
  39.2 0.0 copy-done.2
  39.2 0.0 copy-done.5
  39.2 0.8 fusion.14
  40.0 1.2 fusion.16
  41.2 67.1 %all-gather.2.cloned.1.call-done = bf16[2048,2048]{1,0:T(8,128)(2,1)} async-done(((bf16[64,2048]{1,0:T(8,128)(2,1)}), bf16[2048,2048]{1,0:T(8,128)(2,1)}) %all-gather.2.cloned.1.call-update) | async-done | bytes 8388624 | tf_op jit(solution)/shard_map/all_gather | solution.py:76
  108.3 4.9 %multiply_reduce_fusion = (f32[128]{0:T(128)S(1)}, f32[128,2048]{1,0:T(8,128)S(1)}) fusion(bf16[128,2048]{0,1:T(8,128)(2,1)} %bitcast.126, bf16[2048,2048]{1,0:T(8,128)(2,1)} %all-gather.2.cloned.1.call-done, bf16[128,2048]{1,0:T(8,128)(2,1)} %param.11), kind=kOutput, calls=%fused_computation.44 | convolution fusion | flops 1074790272 | bytes 10486272 | tf_op jit(solution)/shard_map/dot_general | solution.py:74
  113.2 0.0 copy-done.7
  113.2 1.9 convolution_convert_fusion.1
  115.1 0.0 copy-start.9
  115.1 145.8 %all_to_all.10 = bf16[32,48,2048]{2,1,0:T(8,128)(2,1)S(1)} all-to-all(bf16[32,48,2048]{2,1,0:T(8,128)(2,1)S(1)} %bitcast.120), channel_id=1, replica_groups=mesh['group'=8,'expert'=32] {'expert'}, dimensions={0} | all-to-all | bytes 12582912 | tf_op jit(solution)/shard_map/all_to_all | solution.py:102
  260.9 0.0 copy-done.9
  260.9 6.8 %fusion.1 = f32[1536,1024]{1,0:T(8,128)S(1)} fusion(bf16[1536,2048]{1,0:T(8,128)(2,1)S(1)} %bitcast.122, bf16[1,2048,1024]{2,1,0:T(8,128)(2,1)S(1)} %copy-done.9), kind=kOutput, calls=%fused_computation.12 | convolution fusion | flops 6442450944 | bytes 16777216 | tf_op jit(solution)/shard_map/dot_general | solution.py:52
  267.7 0.0 copy-done
  267.7 5.4 %convolution_convert_fusion = bf16[1536,2048]{1,0:T(8,128)(2,1)} fusion(bf16[1,512,2048]{2,1,0:T(8,128)(2,1)S(1)} %copy-done, f32[1536,1024]{1,0:T(8,128)S(1)} %fusion.1), kind=kOutput, calls=%fused_computation.8 | convolution fusion | flops 3229089792 | bytes 14680064 | tf_op jit(solution)/shard_map/dot_general | solution.py:54
  273.1 7.4 %all-to-all-start.1 = ((bf16[32,48,2048]{2,1,0:T(8,128)(2,1)}), bf16[32,48,2048]{2,1,0:T(8,128)(2,1)}, u32[]{:S(2)}, u32[]{:S(2)}) async-start(bf16[32,48,2048]{2,1,0:T(8,128)(2,1)} %bitcast.121), calls=%async_computation.1 | async-start | bytes 12582912 | tf_op jit(solution)/shard_map/all_to_all | solution.py:105
  280.5 0.0 copy-done.8
  280.6 140.9 %all-to-all-done.1 = bf16[32,48,2048]{2,1,0:T(8,128)(2,1)} async-done(((bf16[32,48,2048]{2,1,0:T(8,128)(2,1)}), bf16[32,48,2048]{2,1,0:T(8,128)(2,1)}, u32[]{:S(2)}, u32[]{:S(2)}) %all-to-all-start.1) | async-done | bytes 6291488 | tf_op jit(solution)/shard_map/all_to_all | solution.py:105
  421.5 5.8 %gather_fusion = bf16[128,2048]{1,0:T(8,128)(2,1)} fusion(bf16[1536,2048]{1,0:T(8,128)(2,1)} %bitcast.24, s32[1024]{0:T(1024)S(1)} %get-tuple-element.45), kind=kCustom, calls=%fused_computation | custom fusion | bytes 1049088 | tf_op jit(solution)/shard_map/gather | solution.py:109
  427.3 5.9 %gather_fusion.1 = bf16[128,2048]{1,0:T(8,128)(2,1)} fusion(bf16[1536,2048]{1,0:T(8,128)(2,1)} %bitcast.24, s32[1024]{0:T(1024)S(1)} %get-tuple-element.44), kind=kCustom, calls=%fused_computation.1 | custom fusion | bytes 1049088 | tf_op jit(solution)/shard_map/gather | solution.py:109
  433.2 5.9 %gather_fusion.2 = bf16[128,2048]{1,0:T(8,128)(2,1)} fusion(bf16[1536,2048]{1,0:T(8,128)(2,1)} %bitcast.24, s32[1024]{0:T(1024)S(1)} %get-tuple-element.43), kind=kCustom, calls=%fused_computation.2 | custom fusion | bytes 1049088 | tf_op jit(solution)/shard_map/gather | solution.py:109
  439.1 5.9 %gather_fusion.3 = bf16[128,2048]{1,0:T(8,128)(2,1)} fusion(bf16[1536,2048]{1,0:T(8,128)(2,1)} %bitcast.24, s32[1024]{0:T(1024)S(1)} %get-tuple-element.42), kind=kCustom, calls=%fused_computation.3 | custom fusion | bytes 1049088 | tf_op jit(solution)/shard_map/gather | solution.py:109
  444.9 5.8 %gather_fusion.4 = bf16[128,2048]{1,0:T(8,128)(2,1)} fusion(bf16[1536,2048]{1,0:T(8,128)(2,1)} %bitcast.24, s32[1024]{0:T(1024)S(1)} %get-tuple-element.41), kind=kCustom, calls=%fused_computation.4 | custom fusion | bytes 1049088 | tf_op jit(solution)/shard_map/gather | solution.py:109
  450.7 5.8 %gather_fusion.5 = bf16[128,2048]{1,0:T(8,128)(2,1)} fusion(bf16[1536,2048]{1,0:T(8,128)(2,1)} %bitcast.24, s32[1024]{0:T(1024)S(1)} %get-tuple-element.40), kind=kCustom, calls=%fused_computation.5 | custom fusion | bytes 1049088 | tf_op jit(solution)/shard_map/gather | solution.py:109
  456.6 6.1 %gather_fusion.6 = bf16[128,2048]{1,0:T(8,128)(2,1)} fusion(bf16[1536,2048]{1,0:T(8,128)(2,1)} %bitcast.24, s32[1024]{0:T(1024)S(1)} %get-tuple-element.39), kind=kCustom, calls=%fused_computation.6 | custom fusion | bytes 1049088 | tf_op jit(solution)/shard_map/gather | solution.py:109
  462.6 5.8 %gather_fusion.7 = bf16[128,2048]{1,0:T(8,128)(2,1)} fusion(bf16[1536,2048]{1,0:T(8,128)(2,1)} %bitcast.24, s32[1024]{0:T(1024)S(1)} %get-tuple-element.38), kind=kCustom, calls=%fused_computation.7 | custom fusion | bytes 1049088 | tf_op jit(solution)/shard_map/gather | solution.py:109
  468.5 3.9 add_convert_fusion
  (16 shorter events, 0.1 us)
Async XLA Ops:
  6.5 261.2 %copy-start = (bf16[1,512,2048]{2,1,0:T(8,128)(2,1)S(1)}, bf16[1,512,2048]{2,1,0:T(8,128)(2,1)}, u32[]{:S(2)}) copy-start(bf16[1,512,2048]{2,1,0:T(8,128)(2,1)} %param.21) | copy-start | bytes 6291460
  6.5 101.7 %all-gather.2.cloned.1.call-start = ((), (), s32[]{:S(2)}) async-start(), calls=%async_computation.2 | async-start | bytes 8650752 | tf_op jit(solution)/shard_map/all_gather | solution.py:76
  9.2 27.0 %collective-permute-start = (bf16[1]{0:T(256)(128)(2,1)}, bf16[1]{0:T(256)(128)(2,1)}, u32[]{:S(2)}, u32[]{:S(2)}) collective-permute-start(bf16[1]{0:T(256)(128)(2,1)} %bitcast.8), channel_id=1, source_target_pairs={{0,32},{32,0},{64,96},{96,64},{128,160},{160,128},{192,224},{224,1... | collective-permute-start | bytes 14 | tf_op jit(solution)/shard_map/ppermute | solution.py:20
  13.4 23.5 %collective-permute-start.1 = (bf16[2,128,2048]{1,2,0:T(8,128)(2,1)}, bf16[2,128,2048]{1,2,0:T(8,128)(2,1)}, u32[]{:S(2)}, u32[]{:S(2)}) collective-permute-start(bf16[2,128,2048]{1,2,0:T(8,128)(2,1)} %bitcast.127), channel_id=1, source_target_pairs={{0,32},{32,0},{64,96},{96,64},{128,160},{160,128},{192,224},{224,1... | collective-permute-start | bytes 3145736 | tf_op jit(solution)/shard_map/ppermute | solution.py:20
  17.9 7.8 %copy-start.6 = (s32[128,8]{0,1:T(8,128)S(1)}, s32[128,8]{0,1:T(8,128)}, u32[]{:S(2)}) copy-start(s32[128,8]{0,1:T(8,128)} %param.18) | copy-start | bytes 12292
  34.2 1.4 copy-start.1
  34.2 4.2 copy-start.3
  36.2 3.0 copy-start.4
  36.9 2.3 copy-start.2
  36.9 2.3 copy-start.5
  108.3 5.0 %copy-start.7 = (f32[2048]{0:T(1024)S(1)}, f32[2048]{0:T(1024)}, u32[]{:S(2)}) copy-start(f32[2048]{0:T(1024)} %param.17) | copy-start | bytes 24580
  115.1 145.8 %copy-start.9 = (bf16[1,2048,1024]{2,1,0:T(8,128)(2,1)S(1)}, bf16[1,2048,1024]{2,1,0:T(8,128)(2,1)}, u32[]{:S(2)}) copy-start(bf16[1,2048,1024]{2,1,0:T(8,128)(2,1)} %param.20) | copy-start | bytes 12582916
  273.1 7.4 %copy-start.8 = (f32[128,8]{0,1:T(8,128)S(1)}, f32[128,8]{0,1:T(8,128)}, u32[]{:S(2)}) copy-start(f32[128,8]{0,1:T(8,128)} %param.19) | copy-start | bytes 12292
  273.1 148.4 %all-to-all-start.1 = ((bf16[32,48,2048]{2,1,0:T(8,128)(2,1)}), bf16[32,48,2048]{2,1,0:T(8,128)(2,1)}, u32[]{:S(2)}, u32[]{:S(2)}) async-start(bf16[32,48,2048]{2,1,0:T(8,128)(2,1)} %bitcast.121), calls=%async_computation.1 | async-start | bytes 12582912 | tf_op jit(solution)/shard_map/all_to_all | solution.py:105
Sparse Core Ops, SparseCore 0:
  9.9 98.2 all-gather.1
where the time goes:
time: 489 us; the launch traced here: 479 us
  waiting for transfers between devices  209 us (43%)
  blocking collectives  146 us (30%)
  local copies, waits for them, and re-layouts  66.1 us (14%)
  matrix products  23.3 us (5%)
  between operations  15.3 us (3%)
  other arithmetic  11.2 us (2%)
  starting transfers between devices  8.94 us (2%)
    all_to_all x1, blocking collectives, shards(): lax.all_to_all(outgoing, 'expert', split_axis=0, concat_axis=0, tiled=True)  146 us
    all_to_all x1, waiting for transfers between devices, shards(): lax.all_to_all(output_rows, 'expert', split_axis=0, concat_axis=0, tiled=...  141 us
    all_gather x1, waiting for transfers between devices, shards(): lax.all_gather(o_rows, 'expert', axis=0, tiled=True)  67.1 us
    gather x8, local copies, waits for them, and re-layouts, shards(): picked = returned_rows[flat_slot[:, route_k]].astype(jnp.float32)  47 us
  transfers between devices with their start and end apart: 4, of which 2 were waited for; matrix products, arithmetic and copies ran while one was open for 6% of the time, Pallas kernels for 0%

commit v1 on v0

--- a/solution.py
+++ b/solution.py
@@ -8,6 +8,14 @@
 HD = 128
 FF = 512
 TOPK = 8
+
+
+def gather_from_all(array, axis, dim):
+    count = lax.axis_size(axis)
+    repeats = [count if d == dim else 1 for d in range(array.ndim)]
+    return lax.all_to_all(
+        jnp.tile(array, repeats), axis, split_axis=dim, concat_axis=dim, tiled=True
+    )
 
 
 def swapped(block, axis, distance):
@@ -72,9 +80,7 @@
     part_b = attend(queries, fetched[0], fetched[1], valid_b)
     attended = merge_parts(part_a, part_b)
     projected = jnp.dot(
-        attended,
-        lax.all_gather(o_rows, "expert", axis=0, tiled=True),
-        preferred_element_type=jnp.float32,
+        attended, gather_from_all(o_rows, "expert", 0), preferred_element_type=jnp.float32
     )
     residual = resid.astype(jnp.float32) + projected
     normed = (

time: 489 us -> 576 us (1.18); the launches traced: 479 us -> 573 us
  waiting for transfers between devices: 209 us -> 298 us
  between operations: 15.3 us -> 1.98 us
  starting transfers between devices: 8.94 us -> 20.1 us
    all_to_all x0 -> x1, waiting for transfers between devices: none -> 158 us  [gather_from_all(): lax.all_to_all(jnp.tile(array, repeats), axis, split_axis=dim, concat_axi...]
    all_gather x1 -> x0, waiting for transfers between devices: 67.1 us -> none  [shards(): lax.all_gather(o_rows, 'expert', axis=0, tiled=True)]
    all_to_all x0 -> x1, starting transfers between devices: none -> 11 us  [gather_from_all(): lax.all_to_all(jnp.tile(array, repeats), axis, split_axis=dim, concat_axi...]
  transfers between devices with their start and end apart: 4 -> 4, of which waited for: 2 -> 2; matrix products, arithmetic and copies ran while one was open for 6% -> 5% of each run, Pallas kernels for 0% -> 0%
where the time goes in v1:
time: 576 us; the launch traced here: 573 us
  waiting for transfers between devices  298 us (52%)
  blocking collectives  148 us (26%)
  local copies, waits for them, and re-layouts  69.3 us (12%)
  matrix products  23.4 us (4%)
  starting transfers between devices  20.1 us (3%)
  other arithmetic  11.2 us (2%)
    all_to_all x1, waiting for transfers between devices, gather_from_all(): lax.all_to_all(jnp.tile(array, repeats), axis, split_axis=dim, concat_axi...  158 us
    all_to_all x1, blocking collectives, shards(): lax.all_to_all(outgoing, 'expert', split_axis=0, concat_axis=0, tiled=True)  148 us
    all_to_all x1, waiting for transfers between devices, shards(): lax.all_to_all(output_rows, 'expert', split_axis=0, concat_axis=0, tiled=...  141 us
    gather x8, local copies, waits for them, and re-layouts, shards(): picked = returned_rows[flat_slot[:, route_k]].astype(jnp.float32)  47 us
  transfers between devices with their start and end apart: 4, of which 2 were waited for; matrix products, arithmetic and copies ran while one was open for 5% of the time, Pallas kernels for 0%

profile of v1, /device:TPU:33, one launch (start us, length us, event | category | flops | bytes accessed | tf_op | source)
XLA Modules:
  0.0 572.7 jit_solution(9070720545504948641)
XLA Ops:
  0.0 0.0 copy-start
  0.0 5.4 tile.2
  5.4 0.0 slice-start
  5.4 11.0 %all-to-all-start = ((bf16[32,64,2048]{2,1,0:T(8,128)(2,1)}), bf16[32,64,2048]{2,1,0:T(8,128)(2,1)}, u32[]{:S(2)}, u32[]{:S(2)}) async-start(bf16[32,64,2048]{2,1,0:T(8,128)(2,1)} %tile.2), calls=%async_computation | async-start | bytes 16777216 | tf_op jit(solution)/shard_map/all_to_all | solution.py:16
  16.4 0.0 copy-done.9
  16.4 0.6 fusion.66
  17.6 2.1 collective-permute-start
  19.8 0.0 slice-done
  19.8 1.3 copy.55
  21.1 0.3 collective-permute-start.1
  21.4 2.1 fusion.65
  23.5 1.3 copy.53
  24.8 1.0 copy.39
  25.8 2.3 fusion.63
  28.1 1.3 copy.54
  29.4 1.0 copy.40
  30.4 1.0 copy.35
  31.4 2.0 copy.36
  33.5 0.0 copy-done.6
  33.5 0.1 copy.47
  33.6 0.2 reduce_window_sum.11
  33.8 0.1 copy.49
  33.8 0.6 iota_compare_fusion.2
  34.6 5.6 fusion
  40.1 1.8 bitcast_reduce_fusion
  42.0 0.0 copy-start.1
  42.0 0.0 copy-start.3
  42.0 1.3 copy-done.1
  43.3 0.6 fusion.9
  44.0 0.0 copy-start.4
  44.8 0.0 copy-start.2
  44.8 0.0 copy-start.5
  44.8 0.0 collective-permute-done.1
  44.8 1.4 fusion.64
  46.2 0.0 copy-done.3
  46.2 0.5 fusion.67
  46.8 0.2 fusion.31
  47.0 0.0 copy-done.4
  47.0 0.0 copy-done.2
  47.1 0.0 copy-done.5
  47.1 0.8 fusion.14
  47.8 1.2 fusion.16
  49.0 157.6 %all-to-all-done = bf16[32,64,2048]{2,1,0:T(8,128)(2,1)} async-done(((bf16[32,64,2048]{2,1,0:T(8,128)(2,1)}), bf16[32,64,2048]{2,1,0:T(8,128)(2,1)}, u32[]{:S(2)}, u32[]{:S(2)}) %all-to-all-start) | async-done | bytes 8388640 | tf_op jit(solution)/shard_map/all_to_all | solution.py:16
  206.6 4.9 multiply_reduce_fusion
  211.5 0.0 copy-done.7
  211.6 1.9 convolution_convert_fusion.1
  213.4 0.0 copy-start.10
  213.4 148.4 %all_to_all.19 = bf16[32,48,2048]{2,1,0:T(8,128)(2,1)S(1)} all-to-all(bf16[32,48,2048]{2,1,0:T(8,128)(2,1)S(1)} %bitcast.121), channel_id=1, replica_groups=mesh['group'=8,'expert'=32] {'expert'}, dimensions={0} | all-to-all | bytes 12582912 | tf_op jit(solution)/shard_map/all_to_all | solution.py:108
  361.9 0.0 copy-done.10
  361.9 6.8 %fusion.1 = f32[1536,1024]{1,0:T(8,128)S(1)} fusion(bf16[1536,2048]{1,0:T(8,128)(2,1)S(1)} %bitcast.123, bf16[1,2048,1024]{2,1,0:T(8,128)(2,1)S(1)} %copy-done.10), kind=kOutput, calls=%fused_computation.12 | convolution fusion | flops 6442450944 | bytes 16777216 | tf_op jit(solution)/shard_map/dot_general | solution.py:60
  368.7 0.0 copy-done
  368.7 5.4 convolution_convert_fusion
  374.1 6.7 %all-to-all-start.2 = ((bf16[32,48,2048]{2,1,0:T(8,128)(2,1)}), bf16[32,48,2048]{2,1,0:T(8,128)(2,1)}, u32[]{:S(2)}, u32[]{:S(2)}) async-start(bf16[32,48,2048]{2,1,0:T(8,128)(2,1)} %bitcast.122), calls=%async_computation.2 | async-start | bytes 12582912 | tf_op jit(solution)/shard_map/all_to_all | solution.py:111
  380.9 0.0 copy-done.8
  380.9 140.7 %all-to-all-done.2 = bf16[32,48,2048]{2,1,0:T(8,128)(2,1)} async-done(((bf16[32,48,2048]{2,1,0:T(8,128)(2,1)}), bf16[32,48,2048]{2,1,0:T(8,128)(2,1)}, u32[]{:S(2)}, u32[]{:S(2)}) %all-to-all-start.2) | async-done | bytes 6291488 | tf_op jit(solution)/shard_map/all_to_all | solution.py:111
  521.6 5.8 %gather_fusion = bf16[128,2048]{1,0:T(8,128)(2,1)} fusion(bf16[1536,2048]{1,0:T(8,128)(2,1)} %bitcast.25, s32[1024]{0:T(1024)S(1)} %get-tuple-element.45), kind=kCustom, calls=%fused_computation | custom fusion | bytes 1049088 | tf_op jit(solution)/shard_map/gather | solution.py:115
  527.4 5.9 %gather_fusion.1 = bf16[128,2048]{1,0:T(8,128)(2,1)} fusion(bf16[1536,2048]{1,0:T(8,128)(2,1)} %bitcast.25, s32[1024]{0:T(1024)S(1)} %get-tuple-element.44), kind=kCustom, calls=%fused_computation.1 | custom fusion | bytes 1049088 | tf_op jit(solution)/shard_map/gather | solution.py:115
  533.3 5.9 %gather_fusion.2 = bf16[128,2048]{1,0:T(8,128)(2,1)} fusion(bf16[1536,2048]{1,0:T(8,128)(2,1)} %bitcast.25, s32[1024]{0:T(1024)S(1)} %get-tuple-element.43), kind=kCustom, calls=%fused_computation.2 | custom fusion | bytes 1049088 | tf_op jit(solution)/shard_map/gather | solution.py:115
  539.2 5.9 %gather_fusion.3 = bf16[128,2048]{1,0:T(8,128)(2,1)} fusion(bf16[1536,2048]{1,0:T(8,128)(2,1)} %bitcast.25, s32[1024]{0:T(1024)S(1)} %get-tuple-element.42), kind=kCustom, calls=%fused_computation.3 | custom fusion | bytes 1049088 | tf_op jit(solution)/shard_map/gather | solution.py:115
  545.0 5.8 %gather_fusion.4 = bf16[128,2048]{1,0:T(8,128)(2,1)} fusion(bf16[1536,2048]{1,0:T(8,128)(2,1)} %bitcast.25, s32[1024]{0:T(1024)S(1)} %get-tuple-element.41), kind=kCustom, calls=%fused_computation.4 | custom fusion | bytes 1049088 | tf_op jit(solution)/shard_map/gather | solution.py:115
  550.8 5.8 %gather_fusion.5 = bf16[128,2048]{1,0:T(8,128)(2,1)} fusion(bf16[1536,2048]{1,0:T(8,128)(2,1)} %bitcast.25, s32[1024]{0:T(1024)S(1)} %get-tuple-element.40), kind=kCustom, calls=%fused_computation.5 | custom fusion | bytes 1049088 | tf_op jit(solution)/shard_map/gather | solution.py:115
  556.7 6.1 %gather_fusion.6 = bf16[128,2048]{1,0:T(8,128)(2,1)} fusion(bf16[1536,2048]{1,0:T(8,128)(2,1)} %bitcast.25, s32[1024]{0:T(1024)S(1)} %get-tuple-element.39), kind=kCustom, calls=%fused_computation.6 | custom fusion | bytes 1049088 | tf_op jit(solution)/shard_map/gather | solution.py:115
  562.8 5.8 %gather_fusion.7 = bf16[128,2048]{1,0:T(8,128)(2,1)} fusion(bf16[1536,2048]{1,0:T(8,128)(2,1)} %bitcast.25, s32[1024]{0:T(1024)S(1)} %get-tuple-element.38), kind=kCustom, calls=%fused_computation.7 | custom fusion | bytes 1049088 | tf_op jit(solution)/shard_map/gather | solution.py:115
  568.6 3.9 add_convert_fusion
  (19 shorter events, 0.2 us)
Async XLA Ops:
  0.0 368.7 %copy-start = (bf16[1,512,2048]{2,1,0:T(8,128)(2,1)S(1)}, bf16[1,512,2048]{2,1,0:T(8,128)(2,1)}, u32[]{:S(2)}) copy-start(bf16[1,512,2048]{2,1,0:T(8,128)(2,1)} %param.21) | copy-start | bytes 6291460
  5.4 11.0 %copy-start.9 = (s32[1,2]{1,0:T(1,128)S(1)}, s32[1,2]{1,0:T(1,128)}, u32[]{:S(2)}) copy-start(s32[1,2]{1,0:T(1,128)} %param.15) | copy-start | bytes 28
  5.4 14.4 %slice-start = ((bf16[2,1,2,128,2048]{4,3,2,1,0:T(8,128)(2,1)}), bf16[2,1,1,128,2048]{4,3,2,1,0:T(8,128)(2,1)S(1)}, s32[]{:S(2)}) async-start(bf16[2,1,2,128,2048]{4,3,2,1,0:T(8,128)(2,1)} %param.14), calls=%async_computation.3 | async-start | bytes 2097152 | tf_op jit(solution)/shard_map/slice | solution.py:78
  5.4 201.2 %all-to-all-start = ((bf16[32,64,2048]{2,1,0:T(8,128)(2,1)}), bf16[32,64,2048]{2,1,0:T(8,128)(2,1)}, u32[]{:S(2)}, u32[]{:S(2)}) async-start(bf16[32,64,2048]{2,1,0:T(8,128)(2,1)} %tile.2), calls=%async_computation | async-start | bytes 16777216 | tf_op jit(solution)/shard_map/all_to_all | solution.py:16
  17.6 26.4 %collective-permute-start = (bf16[1]{0:T(256)(128)(2,1)}, bf16[1]{0:T(256)(128)(2,1)}, u32[]{:S(2)}, u32[]{:S(2)}) collective-permute-start(bf16[1]{0:T(256)(128)(2,1)} %bitcast.8), channel_id=1, source_target_pairs={{0,32},{32,0},{64,96},{96,64},{128,160},{160,128},{192,224},{224,1... | collective-permute-start | bytes 14 | tf_op jit(solution)/shard_map/ppermute | solution.py:28
  21.1 23.7 %collective-permute-start.1 = (bf16[2,128,2048]{1,2,0:T(8,128)(2,1)}, bf16[2,128,2048]{1,2,0:T(8,128)(2,1)}, u32[]{:S(2)}, u32[]{:S(2)}) collective-permute-start(bf16[2,128,2048]{1,2,0:T(8,128)(2,1)} %bitcast.128), channel_id=1, source_target_pairs={{0,32},{32,0},{64,96},{96,64},{128,160},{160,128},{192,224},{224,1... | collective-permute-start | bytes 3145736 | tf_op jit(solution)/shard_map/ppermute | solution.py:28
  25.8 7.7 %copy-start.6 = (s32[128,8]{0,1:T(8,128)S(1)}, s32[128,8]{0,1:T(8,128)}, u32[]{:S(2)}) copy-start(s32[128,8]{0,1:T(8,128)} %param.18) | copy-start | bytes 12292
  42.0 1.4 copy-start.1
  42.0 4.2 copy-start.3
  44.0 3.0 copy-start.4
  44.8 2.3 copy-start.2
  44.8 2.3 copy-start.5
  206.6 5.0 copy-start.7
  213.4 148.5 %copy-start.10 = (bf16[1,2048,1024]{2,1,0:T(8,128)(2,1)S(1)}, bf16[1,2048,1024]{2,1,0:T(8,128)(2,1)}, u32[]{:S(2)}) copy-start(bf16[1,2048,1024]{2,1,0:T(8,128)(2,1)} %param.20) | copy-start | bytes 12582916
  374.1 6.8 %copy-start.8 = (f32[128,8]{0,1:T(8,128)S(1)}, f32[128,8]{0,1:T(8,128)}, u32[]{:S(2)}) copy-start(f32[128,8]{0,1:T(8,128)} %param.19) | copy-start | bytes 12292
  374.1 147.5 %all-to-all-start.2 = ((bf16[32,48,2048]{2,1,0:T(8,128)(2,1)}), bf16[32,48,2048]{2,1,0:T(8,128)(2,1)}, u32[]{:S(2)}, u32[]{:S(2)}) async-start(bf16[32,48,2048]{2,1,0:T(8,128)(2,1)} %bitcast.122), calls=%async_computation.2 | async-start | bytes 12582912 | tf_op jit(solution)/shard_map/all_to_all | solution.py:111
